TPU v7x, 32 devices: a whole 2x2x4 slice. The times are simulated.
32 devices in a mesh: branch: 4 (over z), seq: 2 (over x), rep: 4 (over y, core).
Axes of the slice: x: 2, y: 2, z: 4, core: 2. Of those that a mesh axis runs over, the one named last changes fastest.
Arguments:
- noisy: bfloat16 [4, 1024, 5120], P('rep'), may hold values from -6 to 6
- generated: bfloat16 [4, 1024, 5120], P('rep', 'seq'), may hold values from -170 to 170
- caption: bfloat16 [4, 5120], P('rep'), may hold values from -0.59765625 to 0.59765625
- null_caption: bfloat16 [5120], replicated, may hold values from -0.59765625 to 0.59765625
- caption_drop: int32 [4], P('rep'), may hold values from 0 to 1, as said below
- timestep: int32 [4], P('rep'), may hold values from 0 to 999
- window_start: int32 [4], P('rep'), may hold values from 0 to 31736
- teacher_qkv: bfloat16 [3, 5120, 1024], P(None, None, ('branch', 'seq')), may hold values from -0.078125 to 0.078125
- teacher_out: bfloat16 [1024, 5120], P(('branch', 'seq')), may hold values from -0.1875 to 0.1875
- teacher_gain: float32 [5120], replicated, may hold values from 0.5 to 1.5
- teacher_qk_gain: float32 [2, 1024], P(None, ('branch', 'seq')), may hold values from 0.7 to 2.6
- critic_qkv: bfloat16 [3, 5120, 1024], P(None, None, ('branch', 'seq')), may hold values from -0.078125 to 0.078125
- critic_out: bfloat16 [1024, 5120], P(('branch', 'seq')), may hold values from -0.1875 to 0.1875
- critic_gain: float32 [5120], replicated, may hold values from 0.5 to 1.5
- critic_qk_gain: float32 [2, 1024], P(None, ('branch', 'seq')), may hold values from 0.7 to 2.6
Outputs:
- generator_grad: bfloat16 [4, 1024, 5120], P('rep', 'seq')
- critic_qkv_grad: float32 [3, 5120, 1024], P(None, 'rep', ('branch', 'seq'))
- critic_out_grad: float32 [1024, 5120], P(('branch', 'seq'), 'rep')
Inputs may be any that keep to these rules, and one draw needn't show every extreme that they name: `caption_drop`: each window's flag is drawn independently.
All inputs are finite; a program needn't handle non-finite values. Where the computation divides by a largest or mean magnitude, that divisor is 1e-20 or more.
Results may differ from a plain program's by a relative error of at most 0.018.
The roundings to bfloat16 on the way count: a program that leaves them out, or rounds other values in their place, can miss the bound.
Values may be sent and summed in bfloat16 or wider, within the bound.
No kernel may reach another device: no remote copies, remote signals or barrier semaphores. Data moves between devices by JAX's collectives and lax.ppermute only.
A program may use at most 192 MiB of HBM per device.

v0:
```python
import jax
import jax.numpy as jnp
from jax import lax
from jax.sharding import PartitionSpec as P

LEN = 1024
GRID_H = 30
GRID_W = 52
guidance = 5.0
score_scale = 128.0 ** (-0.5)
norm_eps = 1e-06


def rope_tables(first_token):
    token_index = first_token + jnp.arange(LEN, dtype=jnp.int32)
    plane_size = GRID_H * GRID_W
    frame_index = token_index // plane_size
    remainder = token_index - frame_index * plane_size
    row_index = remainder // GRID_W
    column_index = remainder - row_index * GRID_W
    pair_index = jnp.arange(64, dtype=jnp.int32)
    in_frames = pair_index < 22
    in_rows = jnp.logical_and(pair_index >= 22, pair_index < 43)
    local_rank = jnp.where(
        in_frames, pair_index, jnp.where(in_rows, pair_index - 22, pair_index - 43)
    ).astype(jnp.float32)
    axis_width = jnp.where(in_frames, 44.0, 42.0).astype(jnp.float32)
    frequency = jnp.exp(-jnp.log(10000.0) * 2.0 * local_rank / axis_width)
    chosen = jnp.where(
        in_frames[None, :],
        frame_index[:, None],
        jnp.where(in_rows[None, :], row_index[:, None], column_index[:, None]),
    ).astype(jnp.float32)
    angles = chosen * frequency[None, :]
    angles = jnp.concatenate([angles, angles], axis=1)
    return (jnp.cos(angles), jnp.sin(angles))


def rotate_half(values):
    return jnp.concatenate([-values[..., 64:], values[..., :64]], axis=-1)


def rotate_back(values):
    return jnp.concatenate([values[..., 64:], -values[..., :64]], axis=-1)


def norm_tokens(inputs, gain_values):
    scaled = (
        inputs
        * lax.rsqrt(jnp.mean(inputs * inputs, axis=-1, keepdims=True) + norm_eps)
        * gain_values
    )
    return scaled.astype(jnp.bfloat16)


def undo_norm(raw_values, inverse, gain_values, grad_normed):
    scaled = gain_values * grad_normed
    return inverse * scaled - raw_values * inverse * inverse * inverse * jnp.mean(
        scaled * raw_values, axis=-1, keepdims=True
    )


def head_forward(hidden, weights, qk_gains, cosine_table, sine_table):
    projected = jnp.einsum("bsd,kdc->kbsc", hidden, weights, preferred_element_type=jnp.float32)
    batch_size = hidden.shape[0]
    length = hidden.shape[1]
    query_raw = projected[0].reshape(batch_size, length, -1, 128)
    key_raw = projected[1].reshape(batch_size, length, -1, 128)
    value_rows = projected[2].reshape(batch_size, length, -1, 128).astype(jnp.bfloat16)
    gain_query = qk_gains[0].reshape(-1, 128)
    gain_key = qk_gains[1].reshape(-1, 128)
    inv_query = lax.rsqrt(jnp.mean(query_raw * query_raw, axis=-1, keepdims=True) + norm_eps)
    inv_key = lax.rsqrt(jnp.mean(key_raw * key_raw, axis=-1, keepdims=True) + norm_eps)
    normed_query = query_raw * inv_query * gain_query
    normed_key = key_raw * inv_key * gain_key
    cosine_h = cosine_table[:, :, None, :]
    sine_h = sine_table[:, :, None, :]
    rope_query = (normed_query * cosine_h + rotate_half(normed_query) * sine_h).astype(jnp.bfloat16)
    rope_key = (normed_key * cosine_h + rotate_half(normed_key) * sine_h).astype(jnp.bfloat16)
    scores = (
        jnp.einsum("bqhe,bkhe->bhqk", rope_query, rope_key, preferred_element_type=jnp.float32)
        * score_scale
    )
    exponent = jnp.exp(scores)
    probability = exponent / jnp.sum(exponent, axis=-1, keepdims=True)
    prob_rounded = probability.astype(jnp.bfloat16)
    attended = jnp.einsum(
        "bhqk,bkhe->bqhe", prob_rounded, value_rows, preferred_element_type=jnp.float32
    )
    attended = attended.astype(jnp.bfloat16).reshape(batch_size, length, -1)
    saved_state = (
        query_raw,
        key_raw,
        inv_query,
        inv_key,
        rope_query,
        rope_key,
        value_rows,
        probability,
        prob_rounded,
    )
    return (attended, saved_state)


def head_backward(hidden, grad_attn, saved_state, qk_gains, cosine_table, sine_table):
    (
        query_raw,
        key_raw,
        inv_query,
        inv_key,
        rope_query,
        rope_key,
        value_rows,
        probability,
        prob_rounded,
    ) = saved_state
    batch_size = hidden.shape[0]
    length = hidden.shape[1]
    grad_heads = grad_attn.reshape(batch_size, length, -1, 128)
    grad_prob = jnp.einsum(
        "bqhe,bkhe->bhqk", grad_heads, value_rows, preferred_element_type=jnp.float32
    )
    grad_score = (
        probability
        * (grad_prob - jnp.sum(grad_prob * probability, axis=-1, keepdims=True))
        * score_scale
    )
    grad_score = grad_score.astype(jnp.bfloat16)
    grad_qrot = jnp.einsum(
        "bhqk,bkhe->bqhe", grad_score, rope_key, preferred_element_type=jnp.float32
    )
    grad_krot = jnp.einsum(
        "bhqk,bqhe->bkhe", grad_score, rope_query, preferred_element_type=jnp.float32
    )
    grad_value = jnp.einsum(
        "bhqk,bqhe->bkhe", prob_rounded, grad_heads, preferred_element_type=jnp.float32
    )
    cosine_h = cosine_table[:, :, None, :]
    sine_h = sine_table[:, :, None, :]
    grad_qnorm = grad_qrot * cosine_h + rotate_back(grad_qrot * sine_h)
    grad_knorm = grad_krot * cosine_h + rotate_back(grad_krot * sine_h)
    grad_query = undo_norm(query_raw, inv_query, qk_gains[0].reshape(-1, 128), grad_qnorm)
    grad_key = undo_norm(key_raw, inv_key, qk_gains[1].reshape(-1, 128), grad_knorm)
    grad_stack = jnp.stack(
        [
            grad_query.reshape(batch_size, length, -1),
            grad_key.reshape(batch_size, length, -1),
            grad_value.reshape(batch_size, length, -1),
        ]
    ).astype(jnp.bfloat16)
    return jnp.einsum("bsd,kbsc->kdc", hidden, grad_stack, preferred_element_type=jnp.float32)


def body(
    noisy,
    generated,
    caption,
    null_caption,
    caption_drop,
    timestep,
    window_start,
    teacher_qkv,
    teacher_out,
    teacher_gain,
    teacher_qk_gain,
    critic_qkv,
    critic_out,
    critic_gain,
    critic_qk_gain,
):
    length = noisy.shape[1]
    width = noisy.shape[2]
    fraction = (timestep.astype(jnp.float32) + 1.0) / 1001.0
    noise_level = (5.0 * fraction / (1.0 + 4.0 * fraction))[:, None, None]
    used_caption = jnp.where(caption_drop[:, None] == 1, null_caption[None, :], caption)
    cond_shift = used_caption.astype(jnp.float32)[:, None, :]
    null_shift = null_caption.astype(jnp.float32)[None, None, :]
    latent = noisy.astype(jnp.float32)
    cond_normed = norm_tokens(latent + cond_shift, teacher_gain)
    null_normed = norm_tokens(latent + null_shift, teacher_gain)
    critic_normed = norm_tokens(latent + cond_shift, critic_gain)
    cosine_table, sine_table = jax.vmap(rope_tables)(window_start)
    cond_attn, unused = head_forward(
        cond_normed, teacher_qkv, teacher_qk_gain, cosine_table, sine_table
    )
    null_attn, unused = head_forward(
        null_normed, teacher_qkv, teacher_qk_gain, cosine_table, sine_table
    )
    fake_attn, saved_state = head_forward(
        critic_normed, critic_qkv, critic_qk_gain, cosine_table, sine_table
    )
    share_rows = length // lax.axis_size("seq")
    row_start = lax.axis_index("seq") * share_rows
    target = generated.astype(jnp.float32)
    cond_part = jnp.einsum(
        "bsc,cd->sbd", cond_attn, teacher_out, preferred_element_type=jnp.float32
    )
    null_part = jnp.einsum(
        "bsc,cd->sbd", null_attn, teacher_out, preferred_element_type=jnp.float32
    )
    guided_seq = lax.psum_scatter(
        (guidance * cond_part - (guidance - 1.0) * null_part).astype(jnp.bfloat16),
        "seq",
        scatter_dimension=0,
        tiled=True,
    )
    guided_rows = jnp.transpose(lax.psum(guided_seq, "branch").astype(jnp.float32), (1, 0, 2))
    fake_local = jnp.einsum(
        "bsc,cd->bsd", fake_attn, critic_out, preferred_element_type=jnp.float32
    )
    fake_full = lax.psum(fake_local.astype(jnp.bfloat16), ("branch", "seq")).astype(jnp.float32)
    target_full = lax.all_gather(generated, "seq", axis=1, tiled=True).astype(jnp.float32)
    fake_rows = lax.dynamic_slice_in_dim(fake_full, row_start, share_rows, 1)
    latent_rows = lax.dynamic_slice_in_dim(latent, row_start, share_rows, 1)
    cond_rows = latent_rows + cond_shift
    null_rows = latent_rows + null_shift
    real_velocity = guidance * cond_rows - (guidance - 1.0) * null_rows + guided_rows
    fake_velocity = cond_rows + fake_rows
    real_pred = latent_rows - noise_level * real_velocity
    fake_pred = latent_rows - noise_level * fake_velocity
    fake_pred_full = latent - noise_level * (latent + cond_shift + fake_full)
    cotangent = (-noise_level * (fake_pred_full - target_full) / 64.0).astype(jnp.bfloat16)
    out_grads = jnp.einsum("bsc,bsd->cd", fake_attn, cotangent, preferred_element_type=jnp.float32)
    grad_attn = jnp.einsum(
        "bsd,cd->bsc", cotangent, critic_out, preferred_element_type=jnp.float32
    ).astype(jnp.bfloat16)
    abs_total = lax.psum(jnp.sum(jnp.abs(real_pred - target), axis=(1, 2)), "seq")
    spread = abs_total / (length * width)
    generator_grad = ((fake_pred - real_pred) / (spread[:, None, None] + 1e-05)).astype(
        jnp.bfloat16
    )
    proj_share, out_share = (
        lax.psum_scatter(
            head_backward(
                critic_normed, grad_attn, saved_state, critic_qk_gain, cosine_table, sine_table
            ).astype(jnp.bfloat16),
            "rep",
            scatter_dimension=1,
            tiled=True,
        ).astype(jnp.float32),
        lax.psum_scatter(
            out_grads.astype(jnp.bfloat16), "rep", scatter_dimension=1, tiled=True
        ).astype(jnp.float32),
    )
    return (generator_grad, proj_share, out_share)


def solution(mesh):
    in_specs = (
        P("rep", None, None),
        P("rep", "seq", None),
        P("rep", None),
        P(),
        P("rep"),
        P("rep"),
        P("rep"),
        P(None, None, ("branch", "seq")),
        P(("branch", "seq"), None),
        P(),
        P(None, ("branch", "seq")),
        P(None, None, ("branch", "seq")),
        P(("branch", "seq"), None),
        P(),
        P(None, ("branch", "seq")),
    )
    out_specs = (
        P("rep", "seq", None),
        P(None, "rep", ("branch", "seq")),
        P(("branch", "seq"), "rep"),
    )
    return jax.shard_map(body, mesh=mesh, in_specs=in_specs, out_specs=out_specs, check_vma=False)
```

profile of v0, /device:TPU:0, one launch (start us, length us, event | category | flops | bytes accessed | tf_op | source)
XLA Modules:
  0.0 812.3 jit_solution(154347781953120975)
XLA Ops:
  8.0 0.0 copy-start
  8.0 0.0 all-gather.2.cloned.1.call-start
  8.1 0.7 all-gather.2.cloned.1.call-update
  8.8 0.0 all-reduce.3.cloned.1.call-start
  10.1 6.3 copy.18
  16.6 11.9 %multiply_reduce_fusion = (f32[1024]{0:T(1024)S(1)}, f32[1024]{0:T(1024)S(1)}) fusion(bf16[1,1024,5120]{2,1,0:T(8,128)(2,1)} %param.15, f32[5120]{0:T(1024)S(1)} %convert_element_type.334, f32[5120]{0:T(1024)S(1)} %bitcast.380), kind=kLoop, calls=%fused_computation.3 | loop fusion | flops 36698112 | bytes 10534912 | tf_op jit(solution)/shard_map/reduce_sum | solution.py:50
  28.5 6.9 fusion.10
  35.4 0.1 fusion.108
  35.5 0.1 fusion.105
  35.6 1.1 fusion.157
  36.7 0.2 fusion.111
  36.9 0.9 fusion.153
  37.8 0.9 fusion.155
  38.7 4.3 fusion.26
  43.0 2.0 copy-done.5
  45.1 0.9 fusion.33
  46.0 0.7 copy-done.19
  46.7 5.8 convert_bitcast_fusion
  52.5 0.0 all-reduce.3.cloned.1.call-update
  52.5 0.0 reduce-scatter.4.cloned.1.call-start
  52.6 0.0 slice-start
  52.6 6.4 copy.20
  59.0 10.0 %fusion.5 = f32[1024,384]{0,1:S(1)} fusion(bf16[5120,384]{0,1:T(8,128)(2,1)} %bitcast.378, bf16[1,1024,5120]{2,1,0:T(8,128)(2,1)} %param.15, f32[1024]{0:T(1024)S(1)} %add_rsqrt_fusion.2, f32[5120]{0:T(1024)S(1)} %convert_element_type.334, f32[5120]{0:T(1024)S(1)} %copy-done.31), kind=kOutput, calls=%fused_computation.12 | convolution fusion | flops 4052746240 | bytes 16035840
  69.1 0.1 fusion.96
  69.2 4.3 fusion.2
  73.6 0.1 fusion.102
  73.7 0.3 fusion.103
  74.2 0.7 copy-done.8
  74.9 6.2 fusion.28
  81.1 6.4 fusion.27
  87.5 11.7 %fusion.36 = f32[1024,5120]{1,0:T(8,128)} fusion(bf16[128,5120]{1,0:T(8,128)(2,1)S(1)} %copy-done, f32[1024,1024]{0,1:T(8,128)} %get-tuple-element.54, f32[1024]{0:T(1024)S(1)} %get-tuple-element.53, f32[3,1,1024,128]{2,3,1,0:T(8,128)} %bitcast.375), kind=kOutput, calls=%fused_computation.55 | convolution fusion | flops 1613889536 | bytes 26742784 | tf_op jit(solution)/shard_map/bsc,cd->sbd/dot_general | solution.py:195
  99.2 12.8 %fusion.18 = bf16[1024,1,5120]{2,0,1:T(8,128)(2,1)} fusion(bf16[128,5120]{1,0:T(8,128)(2,1)S(1)} %copy-done, f32[1024,5120]{1,0:T(8,128)} %fusion.36, f32[1024,1024]{0,1:T(8,128)} %get-tuple-element.56, f32[1024]{0:T(1024)S(1)} %get-tuple-element.55, f32[3,1,1024,128]{2,3,1,0:T(8,128)S(1)} %bitcast.371), kind=kOutput, calls=%fused_computation.28 | convolution fusion | flops 1634861056 | bytes 37228544 | tf_op jit(solution)/shard_map/bsc,cd->sbd/dot_general | solution.py:198
  112.1 0.0 reduce-scatter.4.cloned.1.call-update
  112.1 0.0 reduce-scatter.8.cloned.1.call-start
  112.8 30.1 %all-gather.2.cloned.1.call-done = bf16[1,1024,5120]{2,1,0:T(8,128)(2,1)} async-done(((bf16[1,512,5120]{2,1,0:T(8,128)(2,1)}), bf16[1,1024,5120]{2,1,0:T(8,128)(2,1)}) %all-gather.2.cloned.1.call-update) | async-done | bytes 10485776 | tf_op jit(solution)/shard_map/all_gather | solution.py:212
  143.0 339.1 %all-reduce.3.cloned.1.call-done = bf16[1,1024,5120]{2,1,0:T(8,128)(2,1)} async-done(((bf16[1,1024,5120]{2,1,0:T(8,128)(2,1)}), bf16[1,1024,5120]{2,1,0:T(8,128)(2,1)}) %all-reduce.3.cloned.1.call-update) | async-done | bytes 10485776 | tf_op jit(solution)/shard_map/psum | solution.py:211
  482.1 13.9 %fusion.7 = bf16[1024,5120]{1,0:T(8,128)(2,1)S(1)} fusion(bf16[1,1024,5120]{2,1,0:T(8,128)(2,1)} %all-gather.2.cloned.1.call-done, bf16[1,1024,5120]{2,1,0:T(8,128)(2,1)} %param.15, f32[]{:T(128)} %bitcast, f32[]{:T(128)} %bitcast.92, f32[5120]{0:T(1024)S(1)} %bitcast.383, bf16[1,1024,5120]{2,1,0:T(8,128)(2,1)} %all-reduce.3.cloned.1.call-done), kind=kLoop, calls=%fused_computation.13 | loop fusion | flops 57671680 | bytes 41963528 | tf_op jit(solution)/shard_map/reshape.74
  496.1 2.9 convolution_convert_fusion.3
  499.0 1.0 multiply_reduce_fusion.2
  500.1 1.2 multiply_convert_fusion.4
  501.3 2.3 convolution_bitcast_fusion.1
  503.6 3.9 fusion.85
  507.6 2.5 fusion.109
  510.2 2.6 convolution_convert_fusion
  512.8 0.0 reduce-scatter.8.cloned.1.call-update
  512.8 0.0 reduce-scatter.6.cloned.1.call-start
  512.9 3.4 fusion.113
  516.4 3.5 fusion.34
  519.9 0.5 slice-done.4
  520.4 1.4 slice-done.5
  521.8 6.2 fusion.22
  528.0 0.0 reduce-scatter.6.cloned.1.call-update
  528.1 0.0 all-reduce.5.cloned.1.call-start
  528.1 0.0 reduce-scatter.4.cloned.1.call-done
  528.1 0.5 all-reduce.5.cloned.1.call-update
  528.6 13.9 %convert_element_type.317 = f32[1,1024,5120]{2,1,0:T(8,128)} convert(bf16[1,1024,5120]{2,1,0:T(8,128)(2,1)} %param.15) | non-fusion elementwise | flops 5242880 | bytes 31457280 | tf_op jit(solution)/shard_map/convert_element_type | solution.py:178
  542.5 14.5 %convert_element_type.333 = f32[1,1024,5120]{2,1,0:T(8,128)} convert(bf16[1,1024,5120]{2,1,0:T(8,128)(2,1)} %all-reduce.3.cloned.1.call-done) | non-fusion elementwise | flops 5242880 | bytes 31457280 | tf_op jit(solution)/shard_map/convert_element_type | solution.py:211
  557.0 1.9 convert_element_type.369
  558.8 25.3 %reduce-scatter.6.cloned.1.call-done = bf16[3,1280,128]{1,2,0:T(8,128)(2,1)} async-done(((bf16[3,5120,128]{1,2,0:T(8,128)(2,1)}), bf16[3,1280,128]{1,2,0:T(8,128)(2,1)}) %reduce-scatter.6.cloned.1.call-update) | async-done | bytes 983056 | tf_op jit(solution)/shard_map/reduce_scatter | solution.py:233
  584.2 2.8 copy.22
  586.9 188.4 %all-reduce.5.cloned.1.call-done = bf16[1,512,5120]{2,1,0:T(8,128)(2,1)} async-done(((bf16[1,512,5120]{2,1,0:T(8,128)(2,1)}), bf16[1,512,5120]{2,1,0:T(8,128)(2,1)}) %all-reduce.5.cloned.1.call-update) | async-done | bytes 5242896 | tf_op jit(solution)/shard_map/psum | solution.py:207
  775.3 9.9 %abs_reduce_fusion = f32[]{:T(128)} fusion(bf16[1,512,5120]{2,1,0:T(8,128)(2,1)} %param.16, bf16[1,512,5120]{2,1,0:T(8,128)(2,1)} %all-reduce.5.cloned.1.call-done, f32[5120]{0:T(1024)S(1)} %convert_element_type.334, f32[5120]{0:T(1024)S(1)} %bitcast.385, f32[]{:T(128)} %bitcast, f32[1,1024,5120]{2,1,0:T(8,128)} %convert_element_type.317, s32[]{:T(128)S(6)} %select_n.143), kind=kLoop, calls=%fused_computation.19 | loop fusion | flops 34078720 | bytes 21012492 | tf_op jit(solution)/shard_map/reduce_sum | solution.py:227
  785.2 5.5 psum.23
  791.4 13.3 %divide_convert_fusion = bf16[1,512,5120]{2,1,0:T(8,128)(2,1)} fusion(f32[1,1024,5120]{2,1,0:T(8,128)} %convert_element_type.333, s32[]{:T(128)S(6)} %select_n.143, f32[1,1024,5120]{2,1,0:T(8,128)} %convert_element_type.317, f32[]{:T(128)} %bitcast.88, f32[5120]{0:T(1024)S(1)} %bitcast.386, f32[]{:T(128)} %bitcast, ...), kind=kLoop, calls=%fused_computation.18 | loop fusion | flops 39321600 | bytes 31498252 | tf_op jit(solution)/shard_map/convert_element_type | solution.py:229
  (98 shorter events, 0.6 us)
Async XLA Ops:
  8.0 79.5 %copy-start = (bf16[128,5120]{1,0:T(8,128)(2,1)S(1)}, bf16[128,5120]{1,0:T(8,128)(2,1)}, u32[]{:S(2)}) copy-start(bf16[128,5120]{1,0:T(8,128)(2,1)} %param.23) | copy-start | bytes 3932164
  8.0 2.1 copy-start.27
  8.0 134.9 %all-gather.2.cloned.1.call-start = ((), (), s32[]{:S(2)}) async-start(), calls=%async_computation.6 | async-start | bytes 15728640 | tf_op jit(solution)/shard_map/all_gather | solution.py:212
  8.8 7.7 copy-start.28
  8.8 473.3 %all-reduce.3.cloned.1.call-start = ((), (), s32[]{:S(2)}) async-start(), calls=%async_computation.3 | async-start | bytes 20971520 | tf_op jit(solution)/shard_map/psum | solution.py:211
  16.6 11.9 %copy-start.2 = (bf16[1,1024,5120]{2,1,0:T(8,128)(2,1)S(1)}, bf16[1,1024,5120]{2,1,0:T(8,128)(2,1)}, u32[]{:S(2)}) copy-start(bf16[1,1024,5120]{2,1,0:T(8,128)(2,1)} %param.15) | copy-start | bytes 31457284
  16.6 11.9 %copy-start.32 = (f32[5120]{0:T(1024)S(1)}, f32[5120]{0:T(1024)}, u32[]{:S(2)}) copy-start(f32[5120]{0:T(1024)} %param.28) | copy-start | bytes 61444
  28.5 7.0 copy-start.29
  35.4 7.6 copy-start.3
  36.7 6.3 copy-start.7
  43.0 2.1 copy-start.5
  45.1 1.6 copy-start.21
  46.0 0.7 copy-start.19
  52.5 6.5 copy-start.31
  52.5 475.6 %reduce-scatter.4.cloned.1.call-start = ((), (), s32[]{:S(2)}) async-start(), calls=%async_computation.4 | async-start | bytes 15728640 | tf_op jit(solution)/shard_map/reduce_scatter | solution.py:201
  52.6 16.6 %slice-start = ((s8[10485760]{0:T(1024)(128)(4,1)}), s8[2097152]{0:T(1024)(128)(4,1)S(1)}, s32[]{:S(2)}) async-start(s8[10485760]{0:T(1024)(128)(4,1)} %bitcast.350), calls=%async_computation.9 | async-start | bytes 4194304
  59.0 10.2 %slice-start.1 = ((s8[10485760]{0:T(1024)(128)(4,1)}), s8[4194304]{0:T(1024)(128)(4,1)S(1)}, s32[]{:S(2)}) async-start(s8[10485760]{0:T(1024)(128)(4,1)} %bitcast.350), calls=%async_computation.10 | async-start | bytes 8388608
  59.0 10.2 %slice-start.2 = ((s8[10485760]{0:T(1024)(128)(4,1)}), s8[4194304]{0:T(1024)(128)(4,1)S(1)}, s32[]{:S(2)}) async-start(s8[10485760]{0:T(1024)(128)(4,1)} %bitcast.350), calls=%async_computation.11 | async-start | bytes 8388608
  59.0 10.2 %copy-start.13 = (bf16[3,5120,128]{1,2,0:T(8,128)(2,1)S(1)}, bf16[3,5120,128]{1,2,0:T(8,128)(2,1)}, u32[]{:S(2)}) copy-start(bf16[3,5120,128]{1,2,0:T(8,128)(2,1)} %copy.20) | copy-start | bytes 11796484
  69.0 5.2 copy-start.9
  69.2 4.5 copy-start.30
  73.6 7.5 copy-start.11
  73.7 1.1 copy-start.8
  87.5 11.7 %copy-start.10 = (f32[1024,384]{0,1:S(1)}, f32[1024,384]{0,1}, u32[]{:S(2)}) copy-start(f32[1024,384]{0,1} %copy-done.9) | copy-start | bytes 4718596
  112.1 444.9 %reduce-scatter.8.cloned.1.call-start = ((), (), s32[]{:S(2)}) async-start(), calls=%async_computation.8 | async-start | bytes 1638400 | tf_op jit(solution)/shard_map/reduce_scatter | solution.py:241
  482.1 14.0 %copy-start.22 = (bf16[128,5120]{1,0:T(8,128)(2,1)S(1)}, bf16[128,5120]{1,0:T(8,128)(2,1)}, u32[]{:S(2)}) copy-start(bf16[128,5120]{1,0:T(8,128)(2,1)} %param.27) | copy-start | bytes 3932164
  496.0 2.9 copy-start.4
  496.0 2.9 copy-start.6
  498.9 1.0 copy-start.33
  500.0 1.3 copy-start.18
  500.0 1.3 copy-start.23
  500.0 1.3 copy-start.24
  500.0 3.5 copy-start.12
  500.0 3.5 copy-start.25
  500.0 3.5 copy-start.26
  507.5 2.7 copy-start.20
  507.5 2.6 copy-start.14
  507.6 2.6 copy-start.15
  507.6 2.5 copy-start.16
  507.6 2.5 copy-start.17
  512.8 7.1 slice-start.3
  512.8 71.3 %reduce-scatter.6.cloned.1.call-start = ((), (), s32[]{:S(2)}) async-start(), calls=%async_computation.7 | async-start | bytes 4915200 | tf_op jit(solution)/shard_map/reduce_scatter | solution.py:233
  516.3 4.1 slice-start.4
  516.4 5.4 slice-start.5
  528.1 247.3 %all-reduce.5.cloned.1.call-start = ((), (), s32[]{:S(2)}) async-start(), calls=%async_computation.5 | async-start | bytes 10485760 | tf_op jit(solution)/shard_map/psum | solution.py:207
  791.4 13.3 %copy-start.1 = (bf16[128,5120]{1,0:T(8,128)(2,1)S(1)}, bf16[128,5120]{1,0:T(8,128)(2,1)}, u32[]{:S(2)}) copy-start(bf16[128,5120]{1,0:T(8,128)(2,1)} %param.23) | copy-start | bytes 3932164
Sparse Core Ops, SparseCore 0:
  10.4 132.5 all-gather.1
  145.3 167.4 reduce-scatter.3
  512.9 25.4 reduce-scatter.7
  541.4 42.7 reduce-scatter.5
  586.4 188.9 all-reduce.4
Sparse Core Ops, SparseCore 1:
  52.6 429.5 all-reduce.2
where the time goes:
time: 821 us; the launch traced here: 812 us
  waiting for transfers between devices  584 us (71%)
  matrix products  91.8 us (11%)
  other arithmetic  90.4 us (11%)
  local copies, waits for them, and re-layouts  21 us (3%)
  between operations  19.2 us (2%)
    psum x1, waiting for transfers between devices, body(): lax.psum(fake_local.astype(jnp.bfloat16), ('branch', 'seq'))  339 us
    psum x1, waiting for transfers between devices, body(): lax.psum(guided_seq, 'branch').astype(jnp.float32)  188 us
    all_gather x1, waiting for transfers between devices, body(): lax.all_gather(generated, 'seq', axis=1, tiled=True).astype(jnp.float32)  30.1 us
    reduce_scatter x1, waiting for transfers between devices, body(): lax.psum_scatter(head_backward(critic_normed, grad_attn, saved_state, cri...  25.3 us
    unnamed x3, matrix products  21.2 us
    unnamed x83, local copies, waits for them, and re-layouts  21 us
    dot_general x3, matrix products, head_forward(): jnp.einsum('bqhe,bkhe->bhqk', rope_query, rope_key, preferred_element_typ...  16.9 us
  transfers between devices with their start and end apart: 6, of which 4 were waited for; matrix products, arithmetic and copies ran while one was open for 21% of the time, Pallas kernels for 0%

commit v1 on v0

--- a/solution.py
+++ b/solution.py
@@ -204,7 +204,9 @@
         scatter_dimension=0,
         tiled=True,
     )
-    guided_rows = jnp.transpose(lax.psum(guided_seq, "branch").astype(jnp.float32), (1, 0, 2))
+    guided_rows = jnp.transpose(
+        jnp.sum(lax.all_gather(guided_seq, "branch"), axis=0).astype(jnp.float32), (1, 0, 2)
+    )
     fake_local = jnp.einsum(
         "bsc,cd->bsd", fake_attn, critic_out, preferred_element_type=jnp.float32
     )

time: 821 us -> 1000 us (1.22)
  waiting for transfers between devices: 584 us -> 751 us
  other arithmetic: 90.4 us -> 105 us
    all_gather x0 -> x1, waiting for transfers between devices: none -> 355 us  [body(): lax.all_gather(guided_seq, 'branch')]
    psum x1 -> x0, waiting for transfers between devices: 188 us -> none  [body(): lax.psum(guided_seq, 'branch').astype(jnp.float32)]
    reduce_sum x0 -> x1, other arithmetic: none -> 15 us  [body(): jnp.sum(lax.all_gather(guided_seq, 'branch'), axis=0).astype(jnp.float32)]
  transfers between devices with their start and end apart: 6 -> 6, of which waited for: 4 -> 4; matrix products, arithmetic and copies ran while one was open for 21% -> 18% of each run, Pallas kernels for 0% -> 0%
where the time goes in v1:
time: 1000 us; the launch traced here: 995 us
  waiting for transfers between devices  751 us (75%)
  other arithmetic  105 us (10%)
  matrix products  91.9 us (9%)
  local copies, waits for them, and re-layouts  20.9 us (2%)
  between operations  19.2 us (2%)
    all_gather x1, waiting for transfers between devices, body(): lax.all_gather(guided_seq, 'branch')  355 us
    psum x1, waiting for transfers between devices, body(): lax.psum(fake_local.astype(jnp.bfloat16), ('branch', 'seq'))  339 us
    all_gather x1, waiting for transfers between devices, body(): lax.all_gather(generated, 'seq', axis=1, tiled=True).astype(jnp.float32)  30 us
    reduce_scatter x1, waiting for transfers between devices, body(): lax.psum_scatter(head_backward(critic_normed, grad_attn, saved_state, cri...  25.3 us
    unnamed x3, matrix products  21.2 us
    unnamed x83, local copies, waits for them, and re-layouts  20.9 us
  transfers between devices with their start and end apart: 6, of which 4 were waited for; matrix products, arithmetic and copies ran while one was open for 18% of the time, Pallas kernels for 0%

profile of v1, /device:TPU:0, one launch (start us, length us, event | category | flops | bytes accessed | tf_op | source)
XLA Modules:
  0.0 994.6 jit_solution(12937940880460334313)
XLA Ops:
  8.0 0.0 copy-start
  8.0 0.0 all-gather.4.cloned.1.call-start
  8.1 0.7 all-gather.4.cloned.1.call-update
  8.8 0.0 all-reduce.2.cloned.1.call-start
  10.1 6.3 copy.18
  16.6 11.9 %multiply_reduce_fusion = (f32[1024]{0:T(1024)S(1)}, f32[1024]{0:T(1024)S(1)}) fusion(bf16[1,1024,5120]{2,1,0:T(8,128)(2,1)} %param.15, f32[5120]{0:T(1024)S(1)} %convert_element_type.350, f32[5120]{0:T(1024)S(1)} %bitcast.387), kind=kLoop, calls=%fused_computation.3 | loop fusion | flops 36698112 | bytes 10534912 | tf_op jit(solution)/shard_map/reduce_sum | solution.py:50
  28.5 6.9 fusion.12
  35.4 0.1 fusion.110
  35.5 0.1 fusion.107
  35.6 1.2 fusion.159
  36.8 0.2 fusion.113
  37.0 0.9 fusion.155
  37.8 0.9 fusion.157
  38.7 4.3 fusion.28
  43.0 2.0 copy-done.5
  45.0 0.9 fusion.35
  45.9 0.7 copy-done.19
  46.6 5.8 convert_bitcast_fusion
  52.4 0.0 all-reduce.2.cloned.1.call-update
  52.5 0.0 reduce-scatter.4.cloned.1.call-start
  52.5 6.4 copy.20
  59.0 10.0 %fusion.5 = f32[1024,384]{0,1:S(1)} fusion(bf16[5120,384]{0,1:T(8,128)(2,1)} %bitcast.385, bf16[1,1024,5120]{2,1,0:T(8,128)(2,1)} %param.15, f32[1024]{0:T(1024)S(1)} %add_rsqrt_fusion.2, f32[5120]{0:T(1024)S(1)} %convert_element_type.350, f32[5120]{0:T(1024)S(1)} %copy-done.31), kind=kOutput, calls=%fused_computation.12 | convolution fusion | flops 4052746240 | bytes 16035840
  69.0 0.1 fusion.98
  69.2 4.3 fusion.2
  73.5 0.1 fusion.104
  73.7 0.3 fusion.105
  74.2 0.7 copy-done.8
  74.8 6.2 fusion.30
  81.1 6.4 fusion.29
  87.5 11.7 %fusion.38 = f32[1024,5120]{1,0:T(8,128)} fusion(bf16[128,5120]{1,0:T(8,128)(2,1)S(1)} %copy-done, f32[1024,1024]{0,1:T(8,128)} %get-tuple-element.54, f32[1024]{0:T(1024)S(1)} %get-tuple-element.53, f32[3,1,1024,128]{2,3,1,0:T(8,128)} %bitcast.383), kind=kOutput, calls=%fused_computation.57 | convolution fusion | flops 1613889536 | bytes 26742784 | tf_op jit(solution)/shard_map/bsc,cd->sbd/dot_general | solution.py:195
  99.2 12.9 %fusion.20 = bf16[1024,1,5120]{2,0,1:T(8,128)(2,1)} fusion(bf16[128,5120]{1,0:T(8,128)(2,1)S(1)} %copy-done, f32[1024,5120]{1,0:T(8,128)} %fusion.38, f32[1024,1024]{0,1:T(8,128)} %get-tuple-element.56, f32[1024]{0:T(1024)S(1)} %get-tuple-element.55, f32[3,1,1024,128]{2,3,1,0:T(8,128)S(1)} %bitcast.379), kind=kOutput, calls=%fused_computation.30 | convolution fusion | flops 1634861056 | bytes 37228544 | tf_op jit(solution)/shard_map/bsc,cd->sbd/dot_general | solution.py:198
  112.2 0.0 reduce-scatter.4.cloned.1.call-update
  112.2 0.0 reduce-scatter.8.cloned.1.call-start
  113.0 30.0 %all-gather.4.cloned.1.call-done = bf16[1,1024,5120]{2,1,0:T(8,128)(2,1)} async-done(((bf16[1,512,5120]{2,1,0:T(8,128)(2,1)}), bf16[1,1024,5120]{2,1,0:T(8,128)(2,1)}) %all-gather.4.cloned.1.call-update) | async-done | bytes 10485776 | tf_op jit(solution)/shard_map/all_gather | solution.py:214
  143.0 339.1 %all-reduce.2.cloned.1.call-done = bf16[1,1024,5120]{2,1,0:T(8,128)(2,1)} async-done(((bf16[1,1024,5120]{2,1,0:T(8,128)(2,1)}), bf16[1,1024,5120]{2,1,0:T(8,128)(2,1)}) %all-reduce.2.cloned.1.call-update) | async-done | bytes 10485776 | tf_op jit(solution)/shard_map/psum | solution.py:213
  482.1 13.9 %fusion.7 = bf16[1024,5120]{1,0:T(8,128)(2,1)S(1)} fusion(bf16[1,1024,5120]{2,1,0:T(8,128)(2,1)} %all-gather.4.cloned.1.call-done, bf16[1,1024,5120]{2,1,0:T(8,128)(2,1)} %param.15, f32[]{:T(128)} %bitcast, f32[]{:T(128)} %bitcast.93, f32[5120]{0:T(1024)S(1)} %bitcast.390, bf16[1,1024,5120]{2,1,0:T(8,128)(2,1)} %all-reduce.2.cloned.1.call-done), kind=kLoop, calls=%fused_computation.13 | loop fusion | flops 57671680 | bytes 41963528 | tf_op jit(solution)/shard_map/reshape.74
  496.1 2.9 convolution_convert_fusion.3
  499.0 1.0 multiply_reduce_fusion.2
  500.1 1.2 multiply_convert_fusion.4
  501.3 2.3 convolution_bitcast_fusion.1
  503.6 3.9 fusion.87
  507.6 2.5 fusion.111
  510.2 2.6 convolution_convert_fusion
  512.8 0.0 reduce-scatter.8.cloned.1.call-update
  512.8 0.0 reduce-scatter.6.cloned.1.call-start
  512.9 3.4 fusion.115
  516.4 3.5 fusion.36
  519.9 0.5 slice-done.4
  520.4 1.4 slice-done.5
  521.8 6.2 fusion.24
  528.0 0.0 reduce-scatter.6.cloned.1.call-update
  528.1 0.0 all-gather.6.cloned.1.call-start
  528.1 0.0 reduce-scatter.4.cloned.1.call-done
  528.1 0.5 all-gather.6.cloned.1.call-update
  528.7 13.9 %convert_element_type.333 = f32[1,1024,5120]{2,1,0:T(8,128)} convert(bf16[1,1024,5120]{2,1,0:T(8,128)(2,1)} %param.15) | non-fusion elementwise | flops 5242880 | bytes 31457280 | tf_op jit(solution)/shard_map/convert_element_type | solution.py:178
  542.5 14.5 %convert_element_type.349 = f32[1,1024,5120]{2,1,0:T(8,128)} convert(bf16[1,1024,5120]{2,1,0:T(8,128)(2,1)} %all-reduce.2.cloned.1.call-done) | non-fusion elementwise | flops 5242880 | bytes 31457280 | tf_op jit(solution)/shard_map/convert_element_type | solution.py:213
  557.0 1.9 convert_element_type.387
  558.9 25.3 %reduce-scatter.6.cloned.1.call-done = bf16[3,1280,128]{1,2,0:T(8,128)(2,1)} async-done(((bf16[3,5120,128]{1,2,0:T(8,128)(2,1)}), bf16[3,1280,128]{1,2,0:T(8,128)(2,1)}) %reduce-scatter.6.cloned.1.call-update) | async-done | bytes 983056 | tf_op jit(solution)/shard_map/reduce_scatter | solution.py:235
  584.2 2.8 copy.22
  587.0 355.5 %all-gather.6.cloned.1.call-done = bf16[2048,1,5120]{2,0,1:T(8,128)(2,1)} async-done(((bf16[512,1,5120]{2,0,1:T(8,128)(2,1)}), bf16[2048,1,5120]{2,0,1:T(8,128)(2,1)}) %all-gather.6.cloned.1.call-update) | async-done | bytes 20971536 | tf_op jit(solution)/shard_map/all_gather | solution.py:208
  942.5 15.0 %reduce.21 = bf16[512,5120]{1,0:T(8,128)(2,1)} reduce(bf16[4,512,5120]{2,1,0:T(8,128)(2,1)} %bitcast.375, bf16[]{:T(256)} %constant.91.clone.1), dimensions={0}, to_apply=%region_13.14 | reduce | flops 7864320 | bytes 26214402 | tf_op jit(solution)/shard_map/reduce_sum | solution.py:208
  957.5 9.9 abs_reduce_fusion
  967.4 5.6 psum.15
  973.7 13.3 %divide_convert_fusion = bf16[1,512,5120]{2,1,0:T(8,128)(2,1)} fusion(f32[1,1024,5120]{2,1,0:T(8,128)} %convert_element_type.349, s32[]{:T(128)S(6)} %select_n.143, f32[1,1024,5120]{2,1,0:T(8,128)} %convert_element_type.333, f32[]{:T(128)} %bitcast.89, f32[5120]{0:T(1024)S(1)} %bitcast.393, f32[]{:T(128)} %bitcast, bf16[512,5120]{1,0:T(8,128)(2,1)} %reduce.21, ...), kind=kLoop, calls=%fused_computation.21 | loop fusion | flops 39321600 | bytes 31498252 | tf_op jit(solution)/shard_map/convert_element_type | solution.py:231
  (99 shorter events, 0.6 us)
Async XLA Ops:
  8.0 79.5 %copy-start = (bf16[128,5120]{1,0:T(8,128)(2,1)S(1)}, bf16[128,5120]{1,0:T(8,128)(2,1)}, u32[]{:S(2)}) copy-start(bf16[128,5120]{1,0:T(8,128)(2,1)} %param.23) | copy-start | bytes 3932164
  8.0 2.1 copy-start.27
  8.0 134.9 %all-gather.4.cloned.1.call-start = ((), (), s32[]{:S(2)}) async-start(), calls=%async_computation.5 | async-start | bytes 15728640 | tf_op jit(solution)/shard_map/all_gather | solution.py:214
  8.8 7.7 copy-start.28
  8.8 473.3 %all-reduce.2.cloned.1.call-start = ((), (), s32[]{:S(2)}) async-start(), calls=%async_computation.3 | async-start | bytes 20971520 | tf_op jit(solution)/shard_map/psum | solution.py:213
  16.6 11.9 %copy-start.2 = (bf16[1,1024,5120]{2,1,0:T(8,128)(2,1)S(1)}, bf16[1,1024,5120]{2,1,0:T(8,128)(2,1)}, u32[]{:S(2)}) copy-start(bf16[1,1024,5120]{2,1,0:T(8,128)(2,1)} %param.15) | copy-start | bytes 31457284
  16.6 11.9 %copy-start.32 = (f32[5120]{0:T(1024)S(1)}, f32[5120]{0:T(1024)}, u32[]{:S(2)}) copy-start(f32[5120]{0:T(1024)} %param.28) | copy-start | bytes 61444
  28.5 7.0 copy-start.29
  35.4 7.6 copy-start.3
  36.8 6.3 copy-start.7
  43.0 2.0 copy-start.5
  45.0 1.6 copy-start.21
  45.9 0.7 copy-start.19
  52.5 6.5 copy-start.31
  52.5 475.7 %reduce-scatter.4.cloned.1.call-start = ((), (), s32[]{:S(2)}) async-start(), calls=%async_computation.4 | async-start | bytes 15728640 | tf_op jit(solution)/shard_map/reduce_scatter | solution.py:201
  52.5 16.6 %slice-start = ((s8[10485760]{0:T(1024)(128)(4,1)}), s8[2097152]{0:T(1024)(128)(4,1)S(1)}, s32[]{:S(2)}) async-start(s8[10485760]{0:T(1024)(128)(4,1)} %bitcast.357), calls=%async_computation.9 | async-start | bytes 4194304
  59.0 10.2 %slice-start.1 = ((s8[10485760]{0:T(1024)(128)(4,1)}), s8[4194304]{0:T(1024)(128)(4,1)S(1)}, s32[]{:S(2)}) async-start(s8[10485760]{0:T(1024)(128)(4,1)} %bitcast.357), calls=%async_computation.10 | async-start | bytes 8388608
  59.0 10.2 %slice-start.2 = ((s8[10485760]{0:T(1024)(128)(4,1)}), s8[4194304]{0:T(1024)(128)(4,1)S(1)}, s32[]{:S(2)}) async-start(s8[10485760]{0:T(1024)(128)(4,1)} %bitcast.357), calls=%async_computation.11 | async-start | bytes 8388608
  59.0 10.2 %copy-start.13 = (bf16[3,5120,128]{1,2,0:T(8,128)(2,1)S(1)}, bf16[3,5120,128]{1,2,0:T(8,128)(2,1)}, u32[]{:S(2)}) copy-start(bf16[3,5120,128]{1,2,0:T(8,128)(2,1)} %copy.20) | copy-start | bytes 11796484
  69.0 5.2 copy-start.9
  69.2 4.5 copy-start.30
  73.5 7.6 copy-start.11
  73.7 1.1 copy-start.8
  87.5 11.7 %copy-start.10 = (f32[1024,384]{0,1:S(1)}, f32[1024,384]{0,1}, u32[]{:S(2)}) copy-start(f32[1024,384]{0,1} %copy-done.9) | copy-start | bytes 4718596
  112.2 444.8 %reduce-scatter.8.cloned.1.call-start = ((), (), s32[]{:S(2)}) async-start(), calls=%async_computation.7 | async-start | bytes 1638400 | tf_op jit(solution)/shard_map/reduce_scatter | solution.py:243
  482.1 14.0 %copy-start.22 = (bf16[128,5120]{1,0:T(8,128)(2,1)S(1)}, bf16[128,5120]{1,0:T(8,128)(2,1)}, u32[]{:S(2)}) copy-start(bf16[128,5120]{1,0:T(8,128)(2,1)} %param.27) | copy-start | bytes 3932164
  496.1 2.9 copy-start.4
  496.1 2.9 copy-start.6
  499.0 1.0 copy-start.33
  500.0 1.3 copy-start.18
  500.0 1.3 copy-start.23
  500.0 1.3 copy-start.24
  500.0 3.5 copy-start.12
  500.0 3.5 copy-start.25
  500.1 3.5 copy-start.26
  507.5 2.7 copy-start.20
  507.6 2.6 copy-start.14
  507.6 2.6 copy-start.15
  507.6 2.5 copy-start.16
  507.6 2.5 copy-start.17
  512.8 7.1 slice-start.3
  512.8 71.4 %reduce-scatter.6.cloned.1.call-start = ((), (), s32[]{:S(2)}) async-start(), calls=%async_computation.6 | async-start | bytes 4915200 | tf_op jit(solution)/shard_map/reduce_scatter | solution.py:235
  516.4 4.1 slice-start.4
  516.4 5.4 slice-start.5
  528.1 414.4 %all-gather.6.cloned.1.call-start = ((), (), s32[]{:S(2)}) async-start(), calls=%async_computation.8 | async-start | bytes 26214400 | tf_op jit(solution)/shard_map/all_gather | solution.py:208
  973.7 13.3 %copy-start.1 = (bf16[128,5120]{1,0:T(8,128)(2,1)S(1)}, bf16[128,5120]{1,0:T(8,128)(2,1)}, u32[]{:S(2)}) copy-start(bf16[128,5120]{1,0:T(8,128)(2,1)} %param.23) | copy-start | bytes 3932164
Sparse Core Ops, SparseCore 0:
  10.4 132.5 all-gather.3
  145.3 167.4 reduce-scatter.3
  513.0 25.4 reduce-scatter.7
  541.4 42.7 reduce-scatter.5
  585.6 356.7 all-gather.5
Sparse Core Ops, SparseCore 1:
  52.5 429.5 all-reduce.1
